TPU v7x, 128 devices: a whole 4x4x4 slice. The times are simulated.
128 devices in a mesh: dp: 16 (over y, x_hi, core), rows: 8 (over z, x_lo).
Axes of the slice: x: 4 (x_hi: 2, x_lo: 2; x = x_hi * 2 + x_lo), y: 4, z: 4, core: 2. Of those that a mesh axis runs over, the one named last changes fastest.
Arguments:
- images: bfloat16 [16, 24, 48, 1280], P('dp', 'rows'), may hold values from -6 to 6
- cotangent: bfloat16 [16, 24, 48, 1280], P('dp', 'rows'), may hold values from -6 to 6
- first_weight: bfloat16 [16, 8, 9, 12800], P('dp', 'rows'), may hold values from -0.0546875 to 0.0546875
- second_weight: bfloat16 [16, 8, 9, 12800], P('dp', 'rows'), may hold values from -0.0546875 to 0.0546875
- first_basis: float32 [64, 1280], replicated, may hold values from -0.15625 to 0.15625
- second_basis: float32 [64, 1280], replicated, may hold values from -0.15625 to 0.15625
Outputs:
- block_output: bfloat16 [16, 24, 48, 1280], P('dp', 'rows')
- first_grad: float32 [16, 8, 9, 12800], P('dp', 'rows')
- second_grad: float32 [16, 8, 9, 12800], P('dp', 'rows')
All inputs are finite; a program needn't handle non-finite values.
Results may differ from a plain program's by a relative error of at most 0.014.
Values may be sent and summed in bfloat16 or wider, within the bound.
A program may use at most 192 MiB of HBM per device.

v0:
```python
import math
import jax
import jax.numpy as jnp
from jax import lax
from jax.sharding import PartitionSpec as P

CHANNELS = 1280
GROUPS = 32
LAT_W = 48
BAND = 3
IMG_DEV = 1


def normalize(values):
    full_shape = values.shape
    size_group = CHANNELS // GROUPS
    grouped = values.reshape(full_shape[:-1] + (full_shape[-1] // size_group, size_group))
    center = jnp.mean(grouped, axis=(1, 2, 4), keepdims=True)
    spread = jnp.mean(jnp.square(grouped - center), axis=(1, 2, 4), keepdims=True)
    return ((grouped - center) / jnp.sqrt(spread + 1e-05)).reshape(full_shape)


def activate(values):
    return jax.nn.silu(normalize(values))


def convolve(inputs, kernel, form):
    padded = jnp.pad(inputs, ((0, 0), (1, 1), (1, 1), (0, 0)))
    height = inputs.shape[1]
    width = inputs.shape[2]
    summed = None
    for row_tap in range(3):
        for col_tap in range(3):
            window = padded[:, row_tap : row_tap + height, col_tap : col_tap + width]
            term = jnp.einsum(
                form, window, kernel[row_tap, col_tap], preferred_element_type=jnp.float32
            )
            summed = term if summed is None else summed + term
    return summed


def weight_grad(inputs, grads, form):
    padded = jnp.pad(inputs, ((0, 0), (1, 1), (1, 1), (0, 0)))
    height = inputs.shape[1]
    width = inputs.shape[2]
    taps = []
    for row_tap in range(3):
        row_list = []
        for col_tap in range(3):
            window = padded[:, row_tap : row_tap + height, col_tap : col_tap + width]
            row_list.append(jnp.einsum(form, window, grads, preferred_element_type=jnp.float32))
        taps.append(jnp.stack(row_list))
    return jnp.stack(taps)


def coefficients(raw_grad, basis):
    return jnp.einsum("abcd,rc->abrd", raw_grad, basis, precision=lax.Precision.HIGHEST)


def expand(basis, coefficient):
    return jnp.einsum("rc,abrd->abcd", basis, coefficient, precision=lax.Precision.HIGHEST)


def body(images, cotangent, first_weight, second_weight, first_basis, second_basis):
    dp_width = CHANNELS // lax.axis_size("dp")
    rows_width = CHANNELS // lax.axis_size("rows")
    grad_scale = 1.0 / math.sqrt(
        lax.axis_size("dp") * IMG_DEV * BAND * lax.axis_size("rows") * LAT_W
    )
    whole_images, whole_cotangent = (
        lax.all_gather(images, "rows", axis=1, tiled=True),
        lax.all_gather(cotangent, "rows", axis=1, tiled=True),
    )
    first_flat = lax.all_gather(first_weight, "dp", axis=3, tiled=True)
    first_full = first_flat.reshape(3, 3, CHANNELS, rows_width)
    activated = activate(whole_images.astype(jnp.float32)).astype(jnp.bfloat16)
    first_out = convolve(activated, first_full, "nhwc,cd->nhwd")
    hidden = activate(first_out).astype(jnp.bfloat16)
    second_flat = lax.all_gather(second_weight, "dp", axis=3, tiled=True)
    second_full = second_flat.reshape(3, 3, CHANNELS, rows_width)
    partial_sums = convolve(hidden, second_full, "nhwc,dc->nhwd")
    band_sums = lax.psum_scatter(
        partial_sums.astype(jnp.bfloat16), "rows", scatter_dimension=1, tiled=True
    ).astype(jnp.float32)
    block_output = (images.astype(jnp.float32) + band_sums).astype(jnp.bfloat16)
    hidden_grad = convolve(whole_cotangent, second_full[::-1, ::-1], "nhwc,cd->nhwd")
    unused, pullback = jax.vjp(activate, first_out)
    pre_grad = pullback(hidden_grad)[0].astype(jnp.bfloat16)
    second_terms = weight_grad(hidden, whole_cotangent, "nhwc,nhwd->dc")
    second_shard = lax.psum_scatter(
        second_terms.astype(jnp.bfloat16), "dp", scatter_dimension=2, tiled=True
    ).astype(jnp.float32)
    basis_rows = lax.dynamic_slice_in_dim(
        second_basis, lax.axis_index("rows") * rows_width, rows_width, 1
    )
    second_coeff = jnp.einsum(
        "abdc,rc->abdr", second_shard, basis_rows, precision=lax.Precision.HIGHEST
    )
    second_sums = lax.psum(second_coeff.astype(jnp.bfloat16), "rows").astype(jnp.float32)
    second_back = jnp.einsum(
        "rc,abdr->abdc", basis_rows, second_sums, precision=lax.Precision.HIGHEST
    )
    second_grad = ((second_shard - second_back) * grad_scale).reshape(
        1, 1, 9, dp_width * rows_width
    )
    basis_images = lax.dynamic_slice_in_dim(
        first_basis, lax.axis_index("dp") * dp_width, dp_width, 1
    )
    first_shard = lax.psum_scatter(
        weight_grad(activated, pre_grad, "nhwc,nhwd->cd").astype(jnp.bfloat16),
        "dp",
        scatter_dimension=2,
        tiled=True,
    ).astype(jnp.float32)
    first_sums = lax.psum(
        coefficients(first_shard, basis_images).astype(jnp.bfloat16), "dp"
    ).astype(jnp.float32)
    first_grad = (first_shard - expand(basis_images, first_sums)) * grad_scale
    first_grad = first_grad.reshape(1, 1, 9, dp_width * rows_width)
    return (block_output, first_grad, second_grad)


def solution(mesh):
    return jax.shard_map(
        body,
        mesh=mesh,
        in_specs=(
            P("dp", "rows", None, None),
            P("dp", "rows", None, None),
            P("dp", "rows", None, None),
            P("dp", "rows", None, None),
            P(),
            P(),
        ),
        out_specs=(
            P("dp", "rows", None, None),
            P("dp", "rows", None, None),
            P("dp", "rows", None, None),
        ),
        check_vma=False,
    )
```

profile of v0, /device:TPU:1, one launch (start us, length us, event | category | flops | bytes accessed | tf_op | source)
XLA Modules:
  0.0 784.7 jit_solution(11428268481880192215)
XLA Ops:
  10.0 70.4 %all-gather.5.cloned.1.call-done = bf16[1,24,48,1280]{3,2,0,1:T(8,128)(2,1)} async-done(((bf16[1,3,48,1280]{3,2,0,1:T(8,128)(2,1)}), bf16[1,24,48,1280]{3,2,0,1:T(8,128)(2,1)}) %all-gather.5.cloned.1.call-update) | async-done | bytes 2949136 | tf_op jit(solution)/shard_map/all_gather | solution.py:71
  80.4 2.5 convert_reduce_fusion
  83.3 0.8 fusion.2
  84.5 3.0 multiply_convert_fusion
  87.5 60.4 %all-gather.7.cloned.1.call-done = bf16[1,1,9,204800]{3,2,1,0:T(8,128)(2,1)} async-done(((bf16[1,1,9,12800]{3,2,1,0:T(8,128)(2,1)}), bf16[1,1,9,204800]{3,2,1,0:T(8,128)(2,1)}) %all-gather.7.cloned.1.call-update) | async-done | bytes 3686416 | tf_op jit(solution)/shard_map/all_gather | solution.py:74
  147.9 15.0 %reshape.402 = bf16[3,3,1280,160]{3,2,1,0:T(8,128)(2,1)} reshape(bf16[1,1,9,204800]{3,2,1,0:T(8,128)(2,1)} %all-gather.7.cloned.1.call-done) | data formatting | bytes 7372800 | tf_op jit(solution)/shard_map/reshape | solution.py:75
  162.9 2.2 fusion.185
  165.8 1.0 fusion.190
  166.8 1.0 fusion.193
  167.8 1.0 fusion.196
  168.8 1.0 fusion.211
  169.7 1.0 fusion.199
  170.7 1.0 fusion.202
  171.7 1.0 fusion.205
  172.7 2.0 fusion.332
  175.0 1.5 multiply_reduce_fusion.1
  177.0 35.9 %all-gather.9.cloned.1.call-done = bf16[1,1,9,204800]{3,2,1,0:T(8,128)(2,1)} async-done(((bf16[1,1,9,12800]{3,2,1,0:T(8,128)(2,1)}), bf16[1,1,9,204800]{3,2,1,0:T(8,128)(2,1)}) %all-gather.9.cloned.1.call-update) | async-done | bytes 3686416 | tf_op jit(solution)/shard_map/all_gather | solution.py:79
  213.0 15.4 %reshape.412 = bf16[3,3,1280,160]{3,2,1,0:T(8,128)(2,1)} reshape(bf16[1,1,9,204800]{3,2,1,0:T(8,128)(2,1)} %all-gather.9.cloned.1.call-done) | data formatting | bytes 7372800 | tf_op jit(solution)/shard_map/reshape | solution.py:80
  228.4 51.1 %all-gather.11.cloned.1.call-done = bf16[1,24,48,1280]{3,2,0,1:T(8,128)(2,1)} async-done(((bf16[1,3,48,1280]{3,2,0,1:T(8,128)(2,1)}), bf16[1,24,48,1280]{3,2,0,1:T(8,128)(2,1)}) %all-gather.11.cloned.1.call-update) | async-done | bytes 2949136 | tf_op jit(solution)/shard_map/all_gather | solution.py:72
  279.5 3.0 fusion.13
  283.2 2.9 fusion.235
  286.1 1.0 fusion.232
  287.1 1.0 fusion.229
  288.1 0.9 fusion.214
  289.0 0.9 fusion.226
  289.9 1.0 fusion.223
  290.9 1.0 fusion.220
  292.2 1.6 fusion.262
  295.4 3.0 fusion.158
  299.2 1.3 fusion.160
  300.5 1.1 fusion.161
  302.3 1.1 fusion.162
  303.4 1.0 fusion.163
  305.2 1.0 fusion.165
  306.6 2.0 pad_maximum_fusion
  308.7 12.1 %copy.96 = bf16[3,3,1280,160]{3,1,0,2:T(4,128)(2,1)} copy(bf16[3,3,1280,160]{2,3,1,0:T(8,128)(2,1)} %pad_maximum_fusion) | data formatting | bytes 7372800
  320.8 14.4 %reshape.471 = bf16[1280,1440]{1,0:T(8,128)(2,1)} reshape(bf16[1280,3,3,160]{3,2,1,0:T(4,128)(2,1)} %bitcast.589) | data formatting | bytes 7372800
  335.5 2.7 fusion.149
  344.6 2.1 pad_maximum_fusion.1
  346.7 12.3 %copy.98 = bf16[3,3,1280,160]{3,1,0,2:T(4,128)(2,1)} copy(bf16[3,3,1280,160]{2,3,1,0:T(8,128)(2,1)} %pad_maximum_fusion.1) | data formatting | bytes 7372800
  359.0 14.5 %reshape.473 = bf16[1280,1440]{1,0:T(8,128)(2,1)} reshape(bf16[1280,3,3,160]{3,2,1,0:T(4,128)(2,1)} %bitcast.590) | data formatting | bytes 7372800
  374.1 4.8 fusion.255
  378.9 4.7 fusion.256
  383.6 4.6 fusion.257
  388.2 3.5 fusion.259
  391.7 3.5 fusion.260
  395.2 3.5 fusion.261
  398.7 3.6 fusion.254
  402.2 3.6 fusion.258
  405.8 6.7 reduce-scatter.10.cloned.1.call-done
  412.5 1.7 reshape.472
  414.6 79.6 %reduce-scatter.12.cloned.1.call-done = bf16[80,1440]{1,0:T(8,128)(2,1)} async-done(((bf16[1280,1440]{1,0:T(8,128)(2,1)}), bf16[80,1440]{1,0:T(8,128)(2,1)}) %reduce-scatter.12.cloned.1.call-update) | async-done | bytes 230416
  494.2 1.7 reshape.474
  496.2 1.9 convolution_convert_fusion.1
  498.2 1.6 fusion.245
  500.1 17.7 %fusion.3 = bf16[1,24,48,1280]{3,2,1,0:T(8,128)(2,1)} fusion(f32[24,48,1280]{2,1,0:T(8,128)} %fusion.261, f32[24,48,1280]{2,1,0:T(8,128)} %fusion.260, f32[24,48,1280]{2,1,0:T(8,128)} %fusion.259, f32[24,48,1280]{2,1,0:T(8,128)} %fusion.258, f32[24,48,1280]{2,1,0:T(8,128)} %fusion.257, f32[24,48,1280]{2,1,0:T(8,128)} %fusion.256, ...), kind=kOutput, calls=%fused_computation.9 | convolution fusion | flops 485130240 | bytes 51159040 | tf_op jit(solution)/shard_map/nhwc,dc->nhwd/dot_general | solution.py:35
  517.9 48.0 %all-reduce.8.cloned.1.call-done = bf16[3,3,80,64]{2,3,1,0:T(8,128)(2,1)} async-done(((bf16[3,3,80,64]{2,3,1,0:T(8,128)(2,1)}), bf16[3,3,80,64]{2,3,1,0:T(8,128)(2,1)}) %all-reduce.8.cloned.1.call-update) | async-done | bytes 92176 | tf_op jit(solution)/shard_map/psum | solution.py:99
  565.8 1.6 fusion.238
  567.8 1.6 reshape.470
  569.4 136.4 %all-reduce.6.cloned.1.call-done = bf16[3,3,64,160]{3,2,1,0:T(8,128)(2,1)} async-done(((bf16[3,3,64,160]{3,2,1,0:T(8,128)(2,1)}), bf16[3,3,64,160]{3,2,1,0:T(8,128)(2,1)}) %all-reduce.6.cloned.1.call-update) | async-done | bytes 184336 | tf_op jit(solution)/shard_map/psum | solution.py:115
  705.8 1.6 fusion.240
  707.8 1.6 reshape.469
  709.4 66.8 %reduce-scatter.8.cloned.1.call-done = bf16[1,3,48,1280]{3,2,1,0:T(8,128)(2,1)} async-done(((bf16[1,24,48,1280]{3,2,1,0:T(8,128)(2,1)}), bf16[1,3,48,1280]{3,2,1,0:T(8,128)(2,1)}) %reduce-scatter.8.cloned.1.call-update) | async-done | bytes 368656 | tf_op jit(solution)/shard_map/reduce_scatter | solution.py:82
  776.2 1.8 add_convert_fusion.2
  (98 shorter events, 19.3 us)
Async XLA Ops:
  7.2 491.1 %copy-start = (f32[64,1280]{1,0:T(8,128)S(1)}, f32[64,1280]{1,0:T(8,128)}, u32[]{:S(2)}) copy-start(f32[64,1280]{1,0:T(8,128)} %param.10) | copy-start | bytes 983044
  7.2 73.2 %all-gather.5.cloned.1.call-start = ((), (), s32[]{:S(2)}) async-start(), calls=%async_computation.3 | async-start | bytes 3317760 | tf_op jit(solution)/shard_map/all_gather | solution.py:71
  7.9 140.0 %all-gather.7.cloned.1.call-start = ((), (), s32[]{:S(2)}) async-start(), calls=%async_computation.4 | async-start | bytes 6963200 | tf_op jit(solution)/shard_map/all_gather | solution.py:74
  8.7 204.3 %all-gather.9.cloned.1.call-start = ((), (), s32[]{:S(2)}) async-start(), calls=%async_computation.5 | async-start | bytes 6963200 | tf_op jit(solution)/shard_map/all_gather | solution.py:79
  9.4 270.1 %all-gather.11.cloned.1.call-start = ((), (), s32[]{:S(2)}) async-start(), calls=%async_computation.7 | async-start | bytes 3317760 | tf_op jit(solution)/shard_map/all_gather | solution.py:72
  10.0 402.6 %reduce-scatter.10.cloned.1.call-start = ((), (), s32[]{:S(2)}) async-start(), calls=%async_computation.10 | async-start | bytes 4177920
  80.4 2.8 copy-start.1
  87.5 75.4 %copy-start.3 = (bf16[1,24,48,1280]{3,2,1,0:T(8,128)(2,1)S(1)}, bf16[1,24,48,1280]{3,2,1,0:T(8,128)(2,1)}, u32[]{:S(2)}) copy-start(bf16[1,24,48,1280]{3,2,1,0:T(8,128)(2,1)} %multiply_convert_fusion) | copy-start | bytes 8847364
  162.9 2.9 copy-start.6
  279.5 3.7 copy-start.2
  283.2 2.9 copy-start.7
  290.9 1.3 copy-start.5
  295.4 3.0 copy-start.4
  335.2 159.0 %reduce-scatter.12.cloned.1.call-start = ((), (), s32[]{:S(2)}) async-start(), calls=%async_computation.11 | async-start | bytes 4177920
  335.5 2.7 copy-start.8
  373.6 192.2 %all-reduce.8.cloned.1.call-start = ((), (), s32[]{:S(2)}) async-start(), calls=%async_computation.9 | async-start | bytes 294912 | tf_op jit(solution)/shard_map/psum | solution.py:99
  374.1 14.1 %slice-start = ((s8[5898240]{0:T(1024)(128)(4,1)}), s8[4194304]{0:T(1024)(128)(4,1)S(1)}, s32[]{:S(2)}) async-start(s8[5898240]{0:T(1024)(128)(4,1)} %bitcast.591), calls=%async_computation.12 | async-start | bytes 8388608
  378.9 9.3 %slice-start.1 = ((s8[5898240]{0:T(1024)(128)(4,1)}), s8[1703936]{0:T(1024)(128)(4,1)S(1)}, s32[]{:S(2)}) async-start(s8[5898240]{0:T(1024)(128)(4,1)} %bitcast.591), calls=%async_computation.13 | async-start | bytes 3407872
  498.2 207.6 %all-reduce.6.cloned.1.call-start = ((), (), s32[]{:S(2)}) async-start(), calls=%async_computation.8 | async-start | bytes 589824 | tf_op jit(solution)/shard_map/psum | solution.py:115
  499.9 276.3 %reduce-scatter.8.cloned.1.call-start = ((), (), s32[]{:S(2)}) async-start(), calls=%async_computation.6 | async-start | bytes 3317760 | tf_op jit(solution)/shard_map/reduce_scatter | solution.py:82
  567.8 208.4 %copy-start.9 = (bf16[1,3,48,1280]{3,2,1,0:T(8,128)(2,1)S(1)}, bf16[1,3,48,1280]{3,2,1,0:T(8,128)(2,1)}, u32[]{:S(2)}) copy-start(bf16[1,3,48,1280]{3,2,1,0:T(8,128)(2,1)} %param.6) | copy-start | bytes 1105924
Sparse Core Ops, SparseCore 0:
  9.6 70.7 all-gather.4
  82.9 64.9 all-gather.6
  150.4 62.5 all-gather.8
  214.5 64.9 all-gather.10
  335.3 77.1 reduce-scatter.9
  416.5 77.5 reduce-scatter.11
  498.3 67.4 all-reduce.7
  568.9 136.8 all-reduce.5
  708.3 67.8 reduce-scatter.7
where the time goes:
time: 794 us; the launch traced here: 785 us
  waiting for transfers between devices  558 us (70%)
  matrix products  99.6 us (13%)
  local copies, waits for them, and re-layouts  95.2 us (12%)
  other arithmetic  16.1 us (2%)
  between operations  14.5 us (2%)
    psum x1, waiting for transfers between devices, body(): lax.psum(coefficients(first_shard, basis_images).astype(jnp.bfloat16), 'dp')  136 us
    unnamed x11, waiting for transfers between devices  89 us
    dot_general x27, matrix products, convolve(): jnp.einsum(form, window, kernel[row_tap, col_tap], preferred_element_type...  73.6 us
    all_gather x1, waiting for transfers between devices, body(): lax.all_gather(images, 'rows', axis=1, tiled=True)  70.4 us
    reduce_scatter x1, waiting for transfers between devices, body(): lax.psum_scatter(partial_sums.astype(jnp.bfloat16), 'rows', scatter_dimen...  66.8 us
    all_gather x1, waiting for transfers between devices, body(): first_flat = lax.all_gather(first_weight, 'dp', axis=3, tiled=True)  60.4 us
    unnamed x32, local copies, waits for them, and re-layouts  59.1 us
    all_gather x1, waiting for transfers between devices, body(): lax.all_gather(cotangent, 'rows', axis=1, tiled=True)  51.1 us
  transfers between devices with their start and end apart: 9, of which 9 were waited for; matrix products, arithmetic and copies ran while one was open for 19% of the time, Pallas kernels for 0%

commit v1 on v0

--- a/solution.py
+++ b/solution.py
@@ -112,8 +112,8 @@
         scatter_dimension=2,
         tiled=True,
     ).astype(jnp.float32)
-    first_sums = lax.psum(
-        coefficients(first_shard, basis_images).astype(jnp.bfloat16), "dp"
+    first_sums = jnp.sum(
+        lax.all_gather(coefficients(first_shard, basis_images).astype(jnp.bfloat16), "dp"), axis=0
     ).astype(jnp.float32)
     first_grad = (first_shard - expand(basis_images, first_sums)) * grad_scale
     first_grad = first_grad.reshape(1, 1, 9, dp_width * rows_width)

time: 794 us -> 719 us (0.906)
  waiting for transfers between devices: 558 us -> 480 us
    psum x1 -> x0, waiting for transfers between devices: 136 us -> none  [body(): lax.psum(coefficients(first_shard, basis_images).astype(jnp.bfloat16), 'dp')]
    all_gather x0 -> x1, waiting for transfers between devices: none -> 58.2 us  [body(): lax.all_gather(coefficients(first_shard, basis_images).astype(jnp.bfloat1...]
    unnamed x11, waiting for transfers between devices: 89 us -> 65.5 us
    psum x1, waiting for transfers between devices: 48 us -> 66.9 us  [body(): lax.psum(second_coeff.astype(jnp.bfloat16), 'rows').astype(jnp.float32)]
    unnamed x32 -> x34, local copies, waits for them, and re-layouts: 59.1 us -> 60.9 us
  transfers between devices with their start and end apart: 9 -> 9, of which waited for: 9 -> 9; matrix products, arithmetic and copies ran while one was open for 19% -> 22% of each run, Pallas kernels for 0% -> 0%
where the time goes in v1:
time: 719 us; the launch traced here: 710 us
  waiting for transfers between devices  480 us (67%)
  matrix products  97.6 us (14%)
  local copies, waits for them, and re-layouts  96.9 us (13%)
  other arithmetic  20.2 us (3%)
  between operations  14.5 us (2%)
    dot_general x27, matrix products, convolve(): jnp.einsum(form, window, kernel[row_tap, col_tap], preferred_element_type...  74.5 us
    reduce_scatter x1, waiting for transfers between devices, body(): lax.psum_scatter(partial_sums.astype(jnp.bfloat16), 'rows', scatter_dimen...  71.3 us
    all_gather x1, waiting for transfers between devices, body(): lax.all_gather(images, 'rows', axis=1, tiled=True)  70.4 us
    psum x1, waiting for transfers between devices, body(): lax.psum(second_coeff.astype(jnp.bfloat16), 'rows').astype(jnp.float32)  66.9 us
    unnamed x11, waiting for transfers between devices  65.5 us
    unnamed x34, local copies, waits for them, and re-layouts  60.9 us
    all_gather x1, waiting for transfers between devices, body(): first_flat = lax.all_gather(first_weight, 'dp', axis=3, tiled=True)  60.3 us
    all_gather x1, waiting for transfers between devices, body(): lax.all_gather(coefficients(first_shard, basis_images).astype(jnp.bfloat1...  58.2 us
  transfers between devices with their start and end apart: 9, of which 9 were waited for; matrix products, arithmetic and copies ran while one was open for 22% of the time, Pallas kernels for 0%

profile of v1, /device:TPU:1, one launch (start us, length us, event | category | flops | bytes accessed | tf_op | source)
XLA Modules:
  0.0 710.0 jit_solution(10857380298417357127)
XLA Ops:
  10.0 70.4 %all-gather.7.cloned.1.call-done = bf16[1,24,48,1280]{3,2,0,1:T(8,128)(2,1)} async-done(((bf16[1,3,48,1280]{3,2,0,1:T(8,128)(2,1)}), bf16[1,24,48,1280]{3,2,0,1:T(8,128)(2,1)}) %all-gather.7.cloned.1.call-update) | async-done | bytes 2949136 | tf_op jit(solution)/shard_map/all_gather | solution.py:71
  80.4 2.5 convert_reduce_fusion
  84.5 3.1 multiply_convert_fusion
  87.5 60.3 %all-gather.9.cloned.1.call-done = bf16[1,1,9,204800]{3,2,1,0:T(8,128)(2,1)} async-done(((bf16[1,1,9,12800]{3,2,1,0:T(8,128)(2,1)}), bf16[1,1,9,204800]{3,2,1,0:T(8,128)(2,1)}) %all-gather.9.cloned.1.call-update) | async-done | bytes 3686416 | tf_op jit(solution)/shard_map/all_gather | solution.py:74
  147.9 15.1 %reshape.402 = bf16[3,3,1280,160]{3,2,1,0:T(8,128)(2,1)} reshape(bf16[1,1,9,204800]{3,2,1,0:T(8,128)(2,1)} %all-gather.9.cloned.1.call-done) | data formatting | bytes 7372800 | tf_op jit(solution)/shard_map/reshape | solution.py:75
  163.0 2.2 fusion.185
  165.9 1.0 fusion.190
  166.8 1.0 fusion.193
  167.8 1.0 fusion.196
  168.8 1.0 fusion.211
  169.8 1.0 fusion.199
  170.7 1.0 fusion.202
  171.7 1.0 fusion.205
  172.7 2.0 fusion.332
  175.1 1.5 multiply_reduce_fusion.1
  177.1 35.9 %all-gather.11.cloned.1.call-done = bf16[1,1,9,204800]{3,2,1,0:T(8,128)(2,1)} async-done(((bf16[1,1,9,12800]{3,2,1,0:T(8,128)(2,1)}), bf16[1,1,9,204800]{3,2,1,0:T(8,128)(2,1)}) %all-gather.11.cloned.1.call-update) | async-done | bytes 3686416 | tf_op jit(solution)/shard_map/all_gather | solution.py:79
  213.0 15.4 %reshape.412 = bf16[3,3,1280,160]{3,2,1,0:T(8,128)(2,1)} reshape(bf16[1,1,9,204800]{3,2,1,0:T(8,128)(2,1)} %all-gather.11.cloned.1.call-done) | data formatting | bytes 7372800 | tf_op jit(solution)/shard_map/reshape | solution.py:80
  228.3 51.2 %all-gather.13.cloned.1.call-done = bf16[1,24,48,1280]{3,2,0,1:T(8,128)(2,1)} async-done(((bf16[1,3,48,1280]{3,2,0,1:T(8,128)(2,1)}), bf16[1,24,48,1280]{3,2,0,1:T(8,128)(2,1)}) %all-gather.13.cloned.1.call-update) | async-done | bytes 2949136 | tf_op jit(solution)/shard_map/all_gather | solution.py:72
  279.5 3.0 fusion.13
  283.2 2.9 fusion.235
  286.1 1.0 fusion.232
  287.1 1.0 fusion.229
  289.0 0.9 fusion.226
  289.9 1.0 fusion.223
  290.9 1.0 fusion.220
  292.2 1.6 fusion.262
  294.9 1.3 add_convert_fusion.1
  299.3 1.0 fusion.131
  304.3 2.0 pad_maximum_fusion.1
  306.4 12.1 %copy.100 = bf16[3,3,1280,160]{3,1,0,2:T(4,128)(2,1)} copy(bf16[3,3,1280,160]{2,3,1,0:T(8,128)(2,1)} %pad_maximum_fusion.1) | data formatting | bytes 7372800
  318.5 14.4 %reshape.474 = bf16[1280,1440]{1,0:T(8,128)(2,1)} reshape(bf16[1280,3,3,160]{3,2,1,0:T(4,128)(2,1)} %bitcast.590) | data formatting | bytes 7372800
  332.9 1.0 copy-done.10
  333.9 3.0 fusion.158
  337.7 1.1 fusion.160
  338.7 1.1 fusion.161
  339.8 1.1 fusion.162
  340.9 1.0 fusion.163
  342.7 1.0 fusion.165
  344.9 2.1 pad_maximum_fusion
  347.0 12.3 %copy.98 = bf16[3,3,1280,160]{3,1,0,2:T(4,128)(2,1)} copy(bf16[3,3,1280,160]{2,3,1,0:T(8,128)(2,1)} %pad_maximum_fusion) | data formatting | bytes 7372800
  359.3 14.5 %reshape.472 = bf16[1280,1440]{1,0:T(8,128)(2,1)} reshape(bf16[1280,3,3,160]{3,2,1,0:T(4,128)(2,1)} %bitcast.591) | data formatting | bytes 7372800
  374.3 4.7 fusion.255
  379.0 4.7 fusion.256
  383.7 4.5 fusion.257
  388.3 3.6 fusion.259
  391.9 3.5 fusion.260
  395.4 3.4 fusion.261
  398.8 3.6 fusion.254
  402.3 3.6 fusion.258
  405.9 4.3 reduce-scatter.12.cloned.1.call-done
  410.2 1.7 reshape.475
  412.2 2.0 convolution_convert_fusion.1
  414.3 18.7 %fusion.3 = bf16[1,24,48,1280]{3,2,1,0:T(8,128)(2,1)} fusion(f32[24,48,1280]{2,1,0:T(8,128)} %fusion.261, f32[24,48,1280]{2,1,0:T(8,128)} %fusion.260, f32[24,48,1280]{2,1,0:T(8,128)} %fusion.259, f32[24,48,1280]{2,1,0:T(8,128)} %fusion.258, f32[24,48,1280]{2,1,0:T(8,128)} %fusion.257, f32[24,48,1280]{2,1,0:T(8,128)} %fusion.256, ...), kind=kOutput, calls=%fused_computation.9 | convolution fusion | flops 485130240 | bytes 51159040 | tf_op jit(solution)/shard_map/nhwc,dc->nhwd/dot_general | solution.py:35
  433.2 58.6 %reduce-scatter.10.cloned.1.call-done = bf16[80,1440]{1,0:T(8,128)(2,1)} async-done(((bf16[1280,1440]{1,0:T(8,128)(2,1)}), bf16[80,1440]{1,0:T(8,128)(2,1)}) %reduce-scatter.10.cloned.1.call-update) | async-done | bytes 230416
  491.9 1.7 reshape.473
  493.9 1.6 fusion.245
  495.5 66.9 %all-reduce.5.cloned.1.call-done = bf16[3,3,80,64]{2,3,1,0:T(8,128)(2,1)} async-done(((bf16[3,3,80,64]{2,3,1,0:T(8,128)(2,1)}), bf16[3,3,80,64]{2,3,1,0:T(8,128)(2,1)}) %all-reduce.5.cloned.1.call-update) | async-done | bytes 92176 | tf_op jit(solution)/shard_map/psum | solution.py:99
  562.4 1.6 fusion.238
  564.4 1.6 reshape.471
  566.0 71.3 %reduce-scatter.8.cloned.1.call-done = bf16[1,3,48,1280]{3,2,1,0:T(8,128)(2,1)} async-done(((bf16[1,24,48,1280]{3,2,1,0:T(8,128)(2,1)}), bf16[1,3,48,1280]{3,2,1,0:T(8,128)(2,1)}) %reduce-scatter.8.cloned.1.call-update) | async-done | bytes 368656 | tf_op jit(solution)/shard_map/reduce_scatter | solution.py:82
  637.3 1.8 add_convert_fusion.2
  639.2 58.2 %all-gather.15.cloned.1.call-done = bf16[48,3,64,160]{3,2,1,0:T(8,128)(2,1)} async-done(((bf16[3,3,64,160]{3,2,1,0:T(8,128)(2,1)}), bf16[48,3,64,160]{3,2,1,0:T(8,128)(2,1)}) %all-gather.15.cloned.1.call-update) | async-done | bytes 2949136 | tf_op jit(solution)/shard_map/all_gather | solution.py:116
  697.4 3.3 reduce_sum.161
  701.6 1.6 reshape.470
  (101 shorter events, 21.7 us)
Async XLA Ops:
  7.2 486.7 %copy-start = (f32[64,1280]{1,0:T(8,128)S(1)}, f32[64,1280]{1,0:T(8,128)}, u32[]{:S(2)}) copy-start(f32[64,1280]{1,0:T(8,128)} %param.10) | copy-start | bytes 983044
  7.2 73.2 %all-gather.7.cloned.1.call-start = ((), (), s32[]{:S(2)}) async-start(), calls=%async_computation.3 | async-start | bytes 3317760 | tf_op jit(solution)/shard_map/all_gather | solution.py:71
  7.9 140.0 %all-gather.9.cloned.1.call-start = ((), (), s32[]{:S(2)}) async-start(), calls=%async_computation.4 | async-start | bytes 6963200 | tf_op jit(solution)/shard_map/all_gather | solution.py:74
  8.7 204.3 %all-gather.11.cloned.1.call-start = ((), (), s32[]{:S(2)}) async-start(), calls=%async_computation.5 | async-start | bytes 6963200 | tf_op jit(solution)/shard_map/all_gather | solution.py:79
  9.4 270.1 %all-gather.13.cloned.1.call-start = ((), (), s32[]{:S(2)}) async-start(), calls=%async_computation.7 | async-start | bytes 3317760 | tf_op jit(solution)/shard_map/all_gather | solution.py:72
  10.0 400.2 %reduce-scatter.12.cloned.1.call-start = ((), (), s32[]{:S(2)}) async-start(), calls=%async_computation.11 | async-start | bytes 4177920
  80.4 2.8 copy-start.1
  87.5 75.4 %copy-start.3 = (bf16[1,24,48,1280]{3,2,1,0:T(8,128)(2,1)S(1)}, bf16[1,24,48,1280]{3,2,1,0:T(8,128)(2,1)}, u32[]{:S(2)}) copy-start(bf16[1,24,48,1280]{3,2,1,0:T(8,128)(2,1)} %multiply_convert_fusion) | copy-start | bytes 8847364
  162.9 2.9 copy-start.6
  279.5 3.7 copy-start.2
  283.2 2.9 copy-start.7
  290.9 1.3 copy-start.5
  294.9 2.1 copy-start.8
  332.8 1.1 copy-start.10
  332.9 159.0 %reduce-scatter.10.cloned.1.call-start = ((), (), s32[]{:S(2)}) async-start(), calls=%async_computation.10 | async-start | bytes 4177920
  333.9 3.0 copy-start.4
  373.8 188.6 %all-reduce.5.cloned.1.call-start = ((), (), s32[]{:S(2)}) async-start(), calls=%async_computation.8 | async-start | bytes 294912 | tf_op jit(solution)/shard_map/psum | solution.py:99
  374.3 14.0 %slice-start = ((s8[5898240]{0:T(1024)(128)(4,1)}), s8[4194304]{0:T(1024)(128)(4,1)S(1)}, s32[]{:S(2)}) async-start(s8[5898240]{0:T(1024)(128)(4,1)} %bitcast.592), calls=%async_computation.12 | async-start | bytes 8388608
  379.0 9.3 %slice-start.1 = ((s8[5898240]{0:T(1024)(128)(4,1)}), s8[1703936]{0:T(1024)(128)(4,1)S(1)}, s32[]{:S(2)}) async-start(s8[5898240]{0:T(1024)(128)(4,1)} %bitcast.592), calls=%async_computation.13 | async-start | bytes 3407872
  414.2 223.1 %reduce-scatter.8.cloned.1.call-start = ((), (), s32[]{:S(2)}) async-start(), calls=%async_computation.6 | async-start | bytes 3317760 | tf_op jit(solution)/shard_map/reduce_scatter | solution.py:82
  433.0 264.3 %all-gather.15.cloned.1.call-start = ((), (), s32[]{:S(2)}) async-start(), calls=%async_computation.9 | async-start | bytes 5013504 | tf_op jit(solution)/shard_map/all_gather | solution.py:116
  493.5 143.8 %copy-start.9 = (bf16[1,3,48,1280]{3,2,1,0:T(8,128)(2,1)S(1)}, bf16[1,3,48,1280]{3,2,1,0:T(8,128)(2,1)}, u32[]{:S(2)}) copy-start(bf16[1,3,48,1280]{3,2,1,0:T(8,128)(2,1)} %param.6) | copy-start | bytes 1105924
Sparse Core Ops, SparseCore 0:
  9.6 70.7 all-gather.6
  82.9 64.9 all-gather.8
  150.4 62.5 all-gather.10
  214.5 64.9 all-gather.12
  333.0 77.1 reduce-scatter.11
  414.2 77.6 reduce-scatter.9
  494.9 67.4 all-reduce.4
  564.9 72.4 reduce-scatter.7
  640.4 56.9 all-gather.14
